TPU v7x, 32 devices: a whole 2x2x4 slice. The times are simulated.
32 devices in a mesh: tiles: 8 (over z, y), freq: 4 (over x, core).
Axes of the slice: x: 2, y: 2, z: 4, core: 2. Of those that a mesh axis runs over, the one named last changes fastest.
Arguments:
- model_in: bfloat16 [4, 1024, 128], P('freq', 'tiles'), may hold values from -6 to 6
- observed: bfloat16 [4, 1024, 128], P('freq', 'tiles'), may hold values from -6 to 6
- right_factors: bfloat16 [4, 8, 2, 256, 128], P('freq', 'tiles'), may hold values from -0.375 to 0.375
- left_factors: bfloat16 [4, 8, 2, 256, 128], P('freq', 'tiles'), may hold values from -0.25 to 0.25
- tile_map: int32 [8, 2], P('tiles'), may hold values from 0 to 3, as said below
- tile_ranks: int32 [4, 8, 2], P('freq', 'tiles'), may hold values from 1 to 64
- window_mix: float32 [4, 4], replicated, may hold values from 0.1 to 0.6
Outputs:
- residual: float32 [4, 1024, 128], P('freq', 'tiles')
- gradient: float32 [4, 1024, 128], P('freq', 'tiles')
Inputs may be any that keep to these rules, and one draw needn't show every extreme that they name: `tile_map`: devices 2j and 2j+1 of tiles together list every tile row 0 to 3 exactly once, 2 distinct rows each. `tile_ranks`: the rank of the tile named by tile_map in the same slot.
All inputs are finite; a program needn't handle non-finite values.
Results may differ from a plain program's by a relative error of at most 0.0042.
Values may be sent and summed in bfloat16 or wider, within the bound.
A program may use at most 64 MiB of HBM per device.

v0:
```python
import jax
import jax.numpy as jnp
from jax import lax
from jax.sharding import PartitionSpec as P


def from_partner(value, axis, apart):
    mask = 2**apart
    pairs = [(source, source ^ mask) for source in range(lax.axis_size(axis))]
    return lax.ppermute(value, axis, pairs)


def conjugate_apply(factor, values):
    product = jnp.einsum("tar,as->trs", factor, values, preferred_element_type=jnp.float32)
    rank_width = factor.shape[2] // 2
    half_cols = values.shape[1] // 2
    real_part = product[:, :rank_width, :half_cols] + product[:, rank_width:, half_cols:]
    imag_part = product[:, :rank_width, half_cols:] - product[:, rank_width:, :half_cols]
    return jnp.concatenate([real_part, imag_part], axis=2)


def factor_apply(factor, coeffs):
    half_cols = coeffs.shape[2] // 2
    real_part = coeffs[:, :, :half_cols]
    imag_part = coeffs[:, :, half_cols:]
    upper_rows = jnp.concatenate([real_part, imag_part], axis=2)
    lower_rows = jnp.concatenate([-imag_part, real_part], axis=2)
    stacked = jnp.concatenate([upper_rows, lower_rows], axis=1)
    return jnp.einsum("tar,trs->as", factor, stacked, preferred_element_type=jnp.float32)


def rank_mask(ranks, rank_width):
    levels = lax.broadcasted_iota(jnp.int32, (ranks.shape[0], rank_width, 1), 1)
    return levels < ranks[:, None, None]


def ordered(parity, mine, theirs):
    first_order = jnp.concatenate([mine, theirs], axis=0)
    second = jnp.concatenate([theirs, mine], axis=0)
    return jnp.where(parity == 0, first_order, second)


def window_step(mixing, freq_index, rows_pred, rows_data):
    weights_row = lax.dynamic_index_in_dim(mixing, freq_index, 0, keepdims=False)
    weights_col = lax.dynamic_index_in_dim(mixing, freq_index, 1, keepdims=False)
    every_pred = lax.all_gather(rows_pred[None], "freq", axis=0, tiled=True)
    residual_rows = (
        jnp.einsum("g,grs->rs", weights_row, every_pred, precision=lax.Precision.HIGHEST)
        - rows_data
    )
    every_res = lax.all_gather(residual_rows[None], "freq", axis=0, tiled=True)
    adjoint_rows = jnp.einsum("g,grs->rs", weights_col, every_res, precision=lax.Precision.HIGHEST)
    return (residual_rows, adjoint_rows)


def body(model_in, observed, right_factors, left_factors, tile_map, tile_ranks, window_mix):
    tile_index = lax.axis_index("tiles")
    parity = tile_index % 2
    tile_count = lax.axis_size("tiles")
    tile_rows = tile_count // 2
    per_device = tile_map.shape[1]
    freq_index = lax.axis_index("freq")
    right_local = right_factors[0, 0]
    left_local = left_factors[0, 0]
    rank_width = right_local.shape[2] // 2
    half_rows = model_in.shape[1]
    width_cols = model_in.shape[2]
    keep_rows = rank_mask(tile_ranks[0, 0], rank_width)
    column_half = tile_index // 2 // per_device
    own_model = model_in[0]
    other_model = from_partner(own_model, "tiles", 0)
    column_block = ordered(parity, own_model, other_model)
    coeffs = jnp.where(keep_rows, conjugate_apply(right_local, column_block), 0.0).astype(
        jnp.bfloat16
    )
    targets = 2 * tile_map[0] + column_half
    outgoing = jnp.zeros((tile_count, rank_width, width_cols), jnp.bfloat16).at[targets].set(coeffs)
    incoming = lax.all_to_all(outgoing, "tiles", split_axis=0, concat_axis=0, tiled=True)
    paired = incoming.reshape(tile_rows, 2, rank_width, width_cols)
    merged = paired[:, 0] + paired[:, 1]
    row_coeffs = lax.dynamic_slice_in_dim(merged, parity * per_device, per_device, 0)
    partial_value = factor_apply(left_local, row_coeffs)
    own_data = observed[0].astype(jnp.float32)
    given_rows = lax.dynamic_slice_in_dim(partial_value, (1 - parity) * half_rows, half_rows, 0)
    received = from_partner(given_rows, "tiles", 0)
    own_pred = lax.dynamic_slice_in_dim(partial_value, parity * half_rows, half_rows, 0) + received
    residual, own_adjoint = window_step(window_mix, freq_index, own_pred, own_data)
    own_bf = own_adjoint.astype(jnp.bfloat16)
    other_bf = from_partner(own_bf, "tiles", 0)
    adjoint_block = ordered(parity, own_bf, other_bf)
    back_coeffs = conjugate_apply(left_local, adjoint_block).astype(jnp.bfloat16)
    doubled = jnp.repeat(back_coeffs, 2, axis=0)
    empty_slots = jnp.zeros((tile_count, rank_width, width_cols), jnp.bfloat16)
    outgoing_back = lax.dynamic_update_slice_in_dim(
        empty_slots, doubled, parity * 2 * per_device, 0
    )
    returned = lax.all_to_all(outgoing_back, "tiles", split_axis=0, concat_axis=0, tiled=True)
    by_row = lax.dynamic_index_in_dim(
        returned.reshape(tile_rows, 2, rank_width, width_cols), column_half, 1, keepdims=False
    )
    picked = jnp.where(keep_rows, by_row[tile_map[0]], 0.0)
    grad_partial = factor_apply(right_local, picked)
    given_grad = lax.dynamic_slice_in_dim(grad_partial, (1 - parity) * half_rows, half_rows, 0)
    received_grad = from_partner(given_grad, "tiles", 0)
    gradient = (
        lax.dynamic_slice_in_dim(grad_partial, parity * half_rows, half_rows, 0) + received_grad
    )
    return (residual[None], gradient[None])


def solution(mesh):
    placed = (
        P("freq", "tiles", None),
        P("freq", "tiles", None),
        P("freq", "tiles", None, None, None),
        P("freq", "tiles", None, None, None),
        P("tiles", None),
        P("freq", "tiles", None),
        P(),
    )
    return jax.shard_map(
        body,
        mesh=mesh,
        in_specs=placed,
        out_specs=(P("freq", "tiles", None), P("freq", "tiles", None)),
        check_vma=False,
    )
```

profile of v0, /device:TPU:0, one launch (start us, length us, event | category | flops | bytes accessed | tf_op | source)
XLA Modules:
  0.0 64.4 jit_solution(17432492704546929525)
XLA Ops:
  0.6 0.0 copy-start
  0.6 3.0 %collective-permute-start = (bf16[128,128]{1,0:T(8,128)(2,1)}, bf16[128,128]{1,0:T(8,128)(2,1)S(1)}, u32[]{:S(2)}, u32[]{:S(2)}) collective-permute-start(bf16[128,128]{1,0:T(8,128)(2,1)} %bitcast.89), channel_id=1, source_target_pairs={{0,4},{4,0},{8,12},{12,8},{16,20},{20,16},{24,28},{28,24},{1,5},{5... | collective-permute-start | bytes 98312 | tf_op jit(solution)/shard_map/ppermute | solution.py:10
  3.7 0.7 %copy-done.5 = s32[1,2]{1,0:T(1,128)S(1)} copy-done((s32[1,2]{1,0:T(1,128)S(1)}, s32[1,2]{1,0:T(1,128)}, u32[]{:S(2)}) %copy-start.5) | copy-done | bytes 32
  4.3 0.7 %copy-done.7 = s32[1,1,2]{2,1,0:T(1,128)S(1)} copy-done((s32[1,1,2]{2,1,0:T(1,128)S(1)}, s32[1,1,2]{2,1,0:T(1,128)}, u32[]{:S(2)}) %copy-start.7) | copy-done | bytes 32
  5.0 0.1 iota_compare_fusion
  5.1 1.0 %copy.13 = bf16[2,256,128]{1,2,0:T(8,128)(2,1)S(1)} copy(bf16[2,256,128]{2,1,0:T(8,128)(2,1)} %bitcast.82) | data formatting | bytes 262144 | tf_op jit(solution)/shard_map/squeeze | solution.py:63
  6.1 0.0 collective-permute-done
  6.1 0.2 fusion.4
  6.3 0.1 slice_add_fusion.1
  6.4 0.1 fusion.10
  6.5 0.7 %broadcast.73.clone = bf16[8,64,128]{2,1,0:T(8,128)(2,1)} broadcast(bf16[]{:T(256)} %constant.63.clone.1), dimensions={} | broadcast | bytes 131074 | tf_op jit(solution)/shard_map/broadcast.8
  7.2 1.9 %scatter_fusion = bf16[8,64,128]{2,1,0:T(8,128)(2,1)} fusion(bf16[8,64,128]{2,1,0:T(8,128)(2,1)} %broadcast.73.clone, s32[2]{0:T(128)S(1)} %get-tuple-element.17, bf16[2,64,128]{2,1,0:T(8,128)(2,1)S(1)} %fusion.10), kind=kCustom, calls=%fused_computation.1 | custom fusion | bytes 98312 | tf_op jit(solution)/shard_map/scatter | solution.py:77
  9.1 6.0 %all-to-all-start = ((bf16[8,64,128]{2,1,0:T(8,128)(2,1)}), bf16[8,64,128]{2,1,0:T(8,128)(2,1)S(1)}, u32[]{:S(2)}, u32[]{:S(2)}) async-start(bf16[8,64,128]{2,1,0:T(8,128)(2,1)} %scatter_fusion), calls=%async_computation | async-start | bytes 262144 | tf_op jit(solution)/shard_map/all_to_all | solution.py:78
  15.1 7.3 %all-to-all-done = bf16[8,64,128]{2,1,0:T(8,128)(2,1)S(1)} async-done(((bf16[8,64,128]{2,1,0:T(8,128)(2,1)}), bf16[8,64,128]{2,1,0:T(8,128)(2,1)S(1)}, u32[]{:S(2)}, u32[]{:S(2)}) %all-to-all-start) | async-done | bytes 131104 | tf_op jit(solution)/shard_map/all_to_all | solution.py:78
  22.5 0.0 copy-start.1
  22.5 0.1 copy.14
  22.6 0.8 %copy-done.1 = bf16[1,1,2,256,128]{4,3,2,1,0:T(8,128)(2,1)S(1)} copy-done((bf16[1,1,2,256,128]{4,3,2,1,0:T(8,128)(2,1)S(1)}, bf16[1,1,2,256,128]{4,3,2,1,0:T(8,128)(2,1)}, u32[]{:S(2)}) %copy-start.1) | copy-done | bytes 131096
  23.4 0.2 convolution_bitcast_fusion.1
  23.6 0.3 collective-permute-start.1
  23.9 0.2 fusion.30
  24.1 3.9 %collective-permute-done.1 = f32[128,128]{0,1:T(8,128)S(1)} collective-permute-done((f32[128,128]{0,1:T(8,128)S(1)}, f32[128,128]{0,1:T(8,128)S(1)}, u32[]{:S(2)}, u32[]{:S(2)}) %collective-permute-start.1) | collective-permute-done | bytes 65568 | tf_op jit(solution)/shard_map/ppermute | solution.py:10
  27.9 5.8 %all-gather = f32[512,128]{0,1:T(8,128)S(1)} all-gather(f32[128,128]{0,1:T(8,128)S(1)} %bitcast_add_fusion.1), channel_id=2, replica_groups=mesh['tiles'=8,'freq'=4] {'freq'}, dimensions={0}, use_global_device_ids=true | all-gather | bytes 327680 | tf_op jit(solution)/shard_map/all_gather | solution.py:46
  33.7 0.1 reshape.112
  33.8 0.6 fusion.32
  34.4 0.0 copy-start.4
  34.4 0.1 copy.18
  34.5 0.7 %copy-done.4 = bf16[1,128,128]{2,1,0:T(8,128)(2,1)S(1)} copy-done((bf16[1,128,128]{2,1,0:T(8,128)(2,1)S(1)}, bf16[1,128,128]{2,1,0:T(8,128)(2,1)}, u32[]{:S(2)}) %copy-start.4) | copy-done | bytes 32792
  35.2 0.0 copy-start.3
  35.2 5.9 %all-gather.1 = f32[512,128]{1,0:T(8,128)S(1)} all-gather(f32[128,128]{1,0:T(8,128)S(1)} %convert_subtract_fusion), channel_id=3, replica_groups=mesh['tiles'=8,'freq'=4] {'freq'}, dimensions={0}, use_global_device_ids=true | all-gather | bytes 327680 | tf_op jit(solution)/shard_map/all_gather | solution.py:51
  41.1 0.7 %fusion = f32[1,128,128]{2,0,1:T(1,128)S(1)} fusion(f32[4,128,128]{2,1,0:T(8,128)S(1)} %bitcast.75, f32[4]{0:T(128)S(1)} %fusion.30), kind=kOutput, calls=%fused_computation.4 | convolution fusion | flops 786432 | bytes 327696 | tf_op jit(solution)/shard_map/g,grs->rs/dot_general | solution.py:52
  41.8 0.3 collective-permute-start.2
  42.0 0.1 copy.15
  42.2 3.6 %collective-permute-done.2 = bf16[128,128]{1,0:T(8,128)(2,1)S(1)} collective-permute-done((bf16[128,128]{1,0:T(8,128)(2,1)S(1)}, bf16[128,128]{1,0:T(8,128)(2,1)S(1)}, u32[]{:S(2)}, u32[]{:S(2)}) %collective-permute-start.2) | collective-permute-done | bytes 32800 | tf_op jit(solution)/shard_map/ppermute | solution.py:10
  45.7 0.2 fusion.16
  45.9 0.1 fusion.3
  46.0 0.1 pad_maximum_fusion
  46.1 0.7 %broadcast.73 = bf16[8,64,128]{2,1,0:T(8,128)(2,1)} broadcast(bf16[]{:T(256)} %constant.63.clone.1), dimensions={} | broadcast | bytes 131074 | tf_op jit(solution)/shard_map/broadcast.8
  46.8 0.6 constant_dynamic-update-slice_fusion
  47.4 3.4 %all-to-all-start.1 = ((bf16[8,64,128]{2,1,0:T(8,128)(2,1)}), bf16[8,64,128]{2,1,0:T(8,128)(2,1)S(1)}, u32[]{:S(2)}, u32[]{:S(2)}) async-start(bf16[8,64,128]{2,1,0:T(8,128)(2,1)} %constant_dynamic-update-slice_fusion), calls=%async_computation.1 | async-start | bytes 262144 | tf_op jit(solution)/shard_map/all_to_all | solution.py:97
  50.8 7.3 %all-to-all-done.1 = bf16[8,64,128]{2,1,0:T(8,128)(2,1)S(1)} async-done(((bf16[8,64,128]{2,1,0:T(8,128)(2,1)}), bf16[8,64,128]{2,1,0:T(8,128)(2,1)S(1)}, u32[]{:S(2)}, u32[]{:S(2)}) %all-to-all-start.1) | async-done | bytes 131104 | tf_op jit(solution)/shard_map/all_to_all | solution.py:97
  58.1 0.6 gather_fusion
  58.7 0.1 broadcast_select_fusion
  58.8 0.1 slice_negate_fusion
  58.8 0.2 copy-done.2
  59.0 0.3 convolution_bitcast_fusion
  59.3 0.3 collective-permute-start.3
  59.6 4.1 %collective-permute-done.3 = f32[128,128]{0,1:T(8,128)S(1)} collective-permute-done((f32[128,128]{0,1:T(8,128)S(1)}, f32[128,128]{0,1:T(8,128)S(1)}, u32[]{:S(2)}, u32[]{:S(2)}) %collective-permute-start.3) | collective-permute-done | bytes 65568 | tf_op jit(solution)/shard_map/ppermute | solution.py:10
  63.6 0.7 %copy.17 = f32[1,128,128]{2,1,0:T(8,128)} copy(f32[1,128,128]{1,2,0:T(8,128)S(1)} %fusion.27) | data formatting | bytes 131072
  (20 shorter events, 0.1 us)
Async XLA Ops:
  0.6 23.2 %copy-start = (f32[4,4]{1,0:T(4,128)S(1)}, f32[4,4]{1,0:T(4,128)}, u32[]{:S(2)}) copy-start(f32[4,4]{1,0:T(4,128)} %param.13) | copy-start | bytes 196
  0.6 5.4 %collective-permute-start = (bf16[128,128]{1,0:T(8,128)(2,1)}, bf16[128,128]{1,0:T(8,128)(2,1)S(1)}, u32[]{:S(2)}, u32[]{:S(2)}) collective-permute-start(bf16[128,128]{1,0:T(8,128)(2,1)} %bitcast.89), channel_id=1, source_target_pairs={{0,4},{4,0},{8,12},{12,8},{16,20},{20,16},{24,28},{28,24},{1,5},{5... | collective-permute-start | bytes 98312 | tf_op jit(solution)/shard_map/ppermute | solution.py:10
  3.7 0.7 %copy-start.5 = (s32[1,2]{1,0:T(1,128)S(1)}, s32[1,2]{1,0:T(1,128)}, u32[]{:S(2)}) copy-start(s32[1,2]{1,0:T(1,128)} %param.11) | copy-start | bytes 28
  4.3 0.7 %copy-start.7 = (s32[1,1,2]{2,1,0:T(1,128)S(1)}, s32[1,1,2]{2,1,0:T(1,128)}, u32[]{:S(2)}) copy-start(s32[1,1,2]{2,1,0:T(1,128)} %param.12) | copy-start | bytes 28
  5.1 1.0 %copy-start.6 = (bf16[1,128,128]{2,1,0:T(8,128)(2,1)S(1)}, bf16[1,128,128]{2,1,0:T(8,128)(2,1)}, u32[]{:S(2)}) copy-start(bf16[1,128,128]{2,1,0:T(8,128)(2,1)} %param.7) | copy-start | bytes 98308
  9.1 13.4 %all-to-all-start = ((bf16[8,64,128]{2,1,0:T(8,128)(2,1)}), bf16[8,64,128]{2,1,0:T(8,128)(2,1)S(1)}, u32[]{:S(2)}, u32[]{:S(2)}) async-start(bf16[8,64,128]{2,1,0:T(8,128)(2,1)} %scatter_fusion), calls=%async_computation | async-start | bytes 262144 | tf_op jit(solution)/shard_map/all_to_all | solution.py:78
  22.5 0.9 %copy-start.1 = (bf16[1,1,2,256,128]{4,3,2,1,0:T(8,128)(2,1)S(1)}, bf16[1,1,2,256,128]{4,3,2,1,0:T(8,128)(2,1)}, u32[]{:S(2)}) copy-start(bf16[1,1,2,256,128]{4,3,2,1,0:T(8,128)(2,1)} %param.10) | copy-start | bytes 393220
  23.6 4.3 %collective-permute-start.1 = (f32[128,128]{0,1:T(8,128)S(1)}, f32[128,128]{0,1:T(8,128)S(1)}, u32[]{:S(2)}, u32[]{:S(2)}) collective-permute-start(f32[128,128]{0,1:T(8,128)S(1)} %dynamic-slice_bitcast_fusion.2), channel_id=1, source_target_pairs={{0,4},{4,0},{8,12},{12,8},{16,20},{20,16},{24,28},{28,24},{1,5},{5... | collective-permute-start | bytes 196616 | tf_op jit(solution)/shard_map/ppermute | solution.py:10
  34.4 0.8 %copy-start.4 = (bf16[1,128,128]{2,1,0:T(8,128)(2,1)S(1)}, bf16[1,128,128]{2,1,0:T(8,128)(2,1)}, u32[]{:S(2)}) copy-start(bf16[1,128,128]{2,1,0:T(8,128)(2,1)} %param.8) | copy-start | bytes 98308
  35.2 5.9 %copy-start.3 = (f32[128,128]{1,0:T(8,128)}, f32[128,128]{1,0:T(8,128)S(1)}, u32[]{:S(2)}) copy-start(f32[128,128]{1,0:T(8,128)S(1)} %convert_subtract_fusion) | copy-start | bytes 196612
  41.8 4.0 %collective-permute-start.2 = (bf16[128,128]{1,0:T(8,128)(2,1)S(1)}, bf16[128,128]{1,0:T(8,128)(2,1)S(1)}, u32[]{:S(2)}, u32[]{:S(2)}) collective-permute-start(bf16[128,128]{1,0:T(8,128)(2,1)S(1)} %convert_element_type.18), channel_id=1, source_target_pairs={{0,4},{4,0},{8,12},{12,8},{16,20},{20,16},{24,28},{28,24},{1,5},{5... | collective-permute-start | bytes 98312 | tf_op jit(solution)/shard_map/ppermute | solution.py:10
  47.4 10.7 %all-to-all-start.1 = ((bf16[8,64,128]{2,1,0:T(8,128)(2,1)}), bf16[8,64,128]{2,1,0:T(8,128)(2,1)S(1)}, u32[]{:S(2)}, u32[]{:S(2)}) async-start(bf16[8,64,128]{2,1,0:T(8,128)(2,1)} %constant_dynamic-update-slice_fusion), calls=%async_computation.1 | async-start | bytes 262144 | tf_op jit(solution)/shard_map/all_to_all | solution.py:97
  58.1 0.9 %copy-start.2 = (bf16[1,1,2,256,128]{4,3,2,1,0:T(8,128)(2,1)S(1)}, bf16[1,1,2,256,128]{4,3,2,1,0:T(8,128)(2,1)}, u32[]{:S(2)}) copy-start(bf16[1,1,2,256,128]{4,3,2,1,0:T(8,128)(2,1)} %param.9) | copy-start | bytes 393220
  59.3 4.3 %collective-permute-start.3 = (f32[128,128]{0,1:T(8,128)S(1)}, f32[128,128]{0,1:T(8,128)S(1)}, u32[]{:S(2)}, u32[]{:S(2)}) collective-permute-start(f32[128,128]{0,1:T(8,128)S(1)} %dynamic-slice_bitcast_fusion), channel_id=1, source_target_pairs={{0,4},{4,0},{8,12},{12,8},{16,20},{20,16},{24,28},{28,24},{1,5},{5... | collective-permute-start | bytes 196616 | tf_op jit(solution)/shard_map/ppermute | solution.py:10
where the time goes:
time: 65 us; the launch traced here: 64.4 us
  waiting for transfers between devices  26.1 us (40%)
  starting transfers between devices  13.2 us (20%)
  blocking collectives  11.7 us (18%)
  local copies, waits for them, and re-layouts  9.71 us (15%)
  matrix products  2.07 us (3%)
  between operations  0.89 us (1%)
  other arithmetic  0.69 us (1%)
    ppermute x4, waiting for transfers between devices, from_partner(): return lax.ppermute(value, axis, pairs)  11.5 us
    all_to_all x1, waiting for transfers between devices, body(): lax.all_to_all(outgoing, 'tiles', split_axis=0, concat_axis=0, tiled=True)  7.34 us
    all_to_all x1, waiting for transfers between devices, body(): lax.all_to_all(outgoing_back, 'tiles', split_axis=0, concat_axis=0, tiled...  7.26 us
    all_to_all x1, starting transfers between devices, body(): lax.all_to_all(outgoing, 'tiles', split_axis=0, concat_axis=0, tiled=True)  6.01 us
    all_gather x1, blocking collectives, window_step(): every_res = lax.all_gather(residual_rows[None], 'freq', axis=0, tiled=True)  5.87 us
    all_gather x1, blocking collectives, window_step(): every_pred = lax.all_gather(rows_pred[None], 'freq', axis=0, tiled=True)  5.79 us
    ppermute x4, starting transfers between devices, from_partner(): return lax.ppermute(value, axis, pairs)  3.86 us
    unnamed x17, local copies, waits for them, and re-layouts  3.63 us
  transfers between devices with their start and end apart: 6, of which 5 were waited for; matrix products, arithmetic and copies ran while one was open for 2% of the time, Pallas kernels for 0%

commit v1 on v0

--- a/solution.py
+++ b/solution.py
@@ -2,6 +2,22 @@
 import jax.numpy as jnp
 from jax import lax
 from jax.sharding import PartitionSpec as P
+
+
+def summed_both_ways(x, axis, dim, term):
+    size, position, span = (lax.axis_size(axis), lax.axis_index(axis), x.shape[dim])
+    forward = [(i, (i + 1) % size) for i in range(size)]
+    downward = [(i, (i - 1) % size) for i in range(size)]
+    half = size // 2
+    from_left = from_right = x
+    total = term(x, position * span)
+    for step in range(1, half + 1):
+        from_left = lax.ppermute(from_left, axis, forward)
+        if step < size - half:
+            from_right = lax.ppermute(from_right, axis, downward)
+            total = total + term(from_right, (position + step) % size * span)
+        total = total + term(from_left, (position - step) % size * span)
+    return total
 
 
 def from_partner(value, axis, apart):
@@ -43,9 +59,18 @@
 def window_step(mixing, freq_index, rows_pred, rows_data):
     weights_row = lax.dynamic_index_in_dim(mixing, freq_index, 0, keepdims=False)
     weights_col = lax.dynamic_index_in_dim(mixing, freq_index, 1, keepdims=False)
-    every_pred = lax.all_gather(rows_pred[None], "freq", axis=0, tiled=True)
     residual_rows = (
-        jnp.einsum("g,grs->rs", weights_row, every_pred, precision=lax.Precision.HIGHEST)
+        summed_both_ways(
+            rows_pred[None],
+            "freq",
+            0,
+            lambda part, offset: jnp.einsum(
+                "g,grs->rs",
+                lax.dynamic_slice_in_dim(weights_row, offset, part.shape[0], axis=0),
+                part,
+                precision=lax.Precision.HIGHEST,
+            ),
+        )
         - rows_data
     )
     every_res = lax.all_gather(residual_rows[None], "freq", axis=0, tiled=True)

time: 65 us -> 67.6 us (1.040)
  blocking collectives: 11.7 us -> 5.79 us
  waiting for transfers between devices: 26.1 us -> 29 us
  other arithmetic: 0.69 us -> 3.18 us
  local copies, waits for them, and re-layouts: 9.71 us -> 11.8 us
  starting transfers between devices: 13.2 us -> 15 us
  matrix products: 2.07 us -> 1.37 us
    all_gather x1 -> x0, blocking collectives: 5.79 us -> none  [window_step(): every_pred = lax.all_gather(rows_pred[None], 'freq', axis=0, tiled=True)]
    ppermute x0 -> x3, waiting for transfers between devices: none -> 3.4 us  [the longest x2 3.39 us: summed_both_ways(): from_left = lax.ppermute(from_left, axis, forward)]
    sub x1, other arithmetic: 0.01 us -> 2.5 us  [window_step(): summed_both_ways(rows_pred[None], 'freq', 0, lambda part, offset: jnp.ein...]
    ppermute x0 -> x3, starting transfers between devices: none -> 1.79 us  [the longest x1 1.73 us: summed_both_ways(): from_right = lax.ppermute(from_right, axis, downward)]
    unnamed x17, local copies, waits for them, and re-layouts: 3.63 us -> 5.12 us
  transfers between devices with their start and end apart: 6 -> 9, of which waited for: 5 -> 7; matrix products, arithmetic and copies ran while one was open for 2% -> 4% of each run, Pallas kernels for 0% -> 0%
where the time goes in v1:
time: 67.6 us; the launch traced here: 67 us
  waiting for transfers between devices  29 us (43%)
  starting transfers between devices  15 us (22%)
  local copies, waits for them, and re-layouts  11.8 us (17%)
  blocking collectives  5.79 us (9%)
  other arithmetic  3.18 us (5%)
  matrix products  1.37 us (2%)
  between operations  0.87 us (1%)
    ppermute x4, waiting for transfers between devices, from_partner(): return lax.ppermute(value, axis, pairs)  11 us
    all_to_all x1, waiting for transfers between devices, body(): lax.all_to_all(outgoing, 'tiles', split_axis=0, concat_axis=0, tiled=True)  7.34 us
    all_to_all x1, waiting for transfers between devices, body(): lax.all_to_all(outgoing_back, 'tiles', split_axis=0, concat_axis=0, tiled...  7.26 us
    all_to_all x1, starting transfers between devices, body(): lax.all_to_all(outgoing, 'tiles', split_axis=0, concat_axis=0, tiled=True)  6.02 us
    all_gather x1, blocking collectives, window_step(): every_res = lax.all_gather(residual_rows[None], 'freq', axis=0, tiled=True)  5.79 us
    unnamed x17, local copies, waits for them, and re-layouts  5.12 us
    ppermute x4, starting transfers between devices, from_partner(): return lax.ppermute(value, axis, pairs)  3.87 us
    ppermute x2, waiting for transfers between devices, summed_both_ways(): from_left = lax.ppermute(from_left, axis, forward)  3.39 us
  transfers between devices with their start and end apart: 9, of which 7 were waited for; matrix products, arithmetic and copies ran while one was open for 4% of the time, Pallas kernels for 0%

profile of v1, /device:TPU:0, one launch (start us, length us, event | category | flops | bytes accessed | tf_op | source)
XLA Modules:
  0.0 67.0 jit_solution(16591217300064009832)
XLA Ops:
  0.6 3.0 %collective-permute-start = (bf16[128,128]{1,0:T(8,128)(2,1)}, bf16[128,128]{1,0:T(8,128)(2,1)S(1)}, u32[]{:S(2)}, u32[]{:S(2)}) collective-permute-start(bf16[128,128]{1,0:T(8,128)(2,1)} %bitcast.104), channel_id=1, source_target_pairs={{0,4},{4,0},{8,12},{12,8},{16,20},{20,16},{24,28},{28,24},{1,5},{5... | collective-permute-start | bytes 98312 | tf_op jit(solution)/shard_map/ppermute | solution.py:26
  3.7 0.7 copy-done.4
  4.3 0.7 copy-done.6
  5.1 1.0 %copy.15 = bf16[2,256,128]{1,2,0:T(8,128)(2,1)S(1)} copy(bf16[2,256,128]{2,1,0:T(8,128)(2,1)} %bitcast.97) | data formatting | bytes 262144 | tf_op jit(solution)/shard_map/squeeze | solution.py:88
  6.1 0.2 fusion.2
  6.3 0.1 slice_add_fusion.1
  6.4 0.1 fusion.8
  6.5 0.7 broadcast.86.clone
  7.2 1.9 %scatter_fusion = bf16[8,64,128]{2,1,0:T(8,128)(2,1)} fusion(bf16[8,64,128]{2,1,0:T(8,128)(2,1)} %broadcast.86.clone, s32[2]{0:T(128)S(1)} %get-tuple-element.21, bf16[2,64,128]{2,1,0:T(8,128)(2,1)S(1)} %fusion.8), kind=kCustom, calls=%fused_computation.1 | custom fusion | bytes 98312 | tf_op jit(solution)/shard_map/scatter | solution.py:102
  9.0 6.0 %all-to-all-start = ((bf16[8,64,128]{2,1,0:T(8,128)(2,1)}), bf16[8,64,128]{2,1,0:T(8,128)(2,1)S(1)}, u32[]{:S(2)}, u32[]{:S(2)}) async-start(bf16[8,64,128]{2,1,0:T(8,128)(2,1)} %scatter_fusion), calls=%async_computation | async-start | bytes 262144 | tf_op jit(solution)/shard_map/all_to_all | solution.py:103
  15.1 7.3 %all-to-all-done = bf16[8,64,128]{2,1,0:T(8,128)(2,1)S(1)} async-done(((bf16[8,64,128]{2,1,0:T(8,128)(2,1)}), bf16[8,64,128]{2,1,0:T(8,128)(2,1)S(1)}, u32[]{:S(2)}, u32[]{:S(2)}) %all-to-all-start) | async-done | bytes 131104 | tf_op jit(solution)/shard_map/all_to_all | solution.py:103
  22.5 0.1 copy.16
  22.6 0.8 %copy-done = bf16[1,1,2,256,128]{4,3,2,1,0:T(8,128)(2,1)S(1)} copy-done((bf16[1,1,2,256,128]{4,3,2,1,0:T(8,128)(2,1)S(1)}, bf16[1,1,2,256,128]{4,3,2,1,0:T(8,128)(2,1)}, u32[]{:S(2)}) %copy-start) | copy-done | bytes 131096
  23.4 0.2 convolution_bitcast_fusion.1
  23.6 0.3 collective-permute-start.1
  23.9 4.1 %collective-permute-done.1 = f32[128,128]{0,1:T(8,128)S(1)} collective-permute-done((f32[128,128]{0,1:T(8,128)S(1)}, f32[128,128]{0,1:T(8,128)S(1)}, u32[]{:S(2)}, u32[]{:S(2)}) %collective-permute-start.1) | collective-permute-done | bytes 65568 | tf_op jit(solution)/shard_map/ppermute | solution.py:26
  28.0 1.7 %collective-permute-start.2 = (f32[1,128,128]{1,2,0:T(8,128)S(1)}, f32[1,128,128]{1,2,0:T(8,128)S(1)}, u32[]{:S(2)}, u32[]{:S(2)}) collective-permute-start(f32[1,128,128]{1,2,0:T(8,128)S(1)} %fusion.28), channel_id=1, source_target_pairs={{0,3},{1,0},{2,1},{3,2},{4,7},{5,4},{6,5},{7,6},{8,11},{9,8},{10,9... | collective-permute-start | bytes 196616 | tf_op jit(solution)/shard_map/ppermute | solution.py:17
  29.7 1.9 %collective-permute-done.3 = f32[1,128,128]{1,2,0:T(8,128)S(1)} collective-permute-done((f32[1,128,128]{1,2,0:T(8,128)S(1)}, f32[1,128,128]{1,2,0:T(8,128)S(1)}, u32[]{:S(2)}, u32[]{:S(2)}) %collective-permute-start.3) | collective-permute-done | bytes 65568 | tf_op jit(solution)/shard_map/ppermute | solution.py:15
  31.7 0.8 %copy-done.2 = bf16[1,128,128]{2,1,0:T(8,128)(2,1)S(1)} copy-done((bf16[1,128,128]{2,1,0:T(8,128)(2,1)S(1)}, bf16[1,128,128]{2,1,0:T(8,128)(2,1)}, u32[]{:S(2)}) %copy-start.2) | copy-done | bytes 32792
  32.4 0.1 copy.17
  32.5 0.6 copy-done.3
  33.1 0.2 fusion.29
  33.3 0.6 fusion.42
  33.9 1.5 %collective-permute-done.4 = f32[1,128,128]{1,2,0:T(8,128)S(1)} collective-permute-done((f32[1,128,128]{1,2,0:T(8,128)S(1)}, f32[1,128,128]{1,2,0:T(8,128)S(1)}, u32[]{:S(2)}, u32[]{:S(2)}) %collective-permute-start.4) | collective-permute-done | bytes 65568 | tf_op jit(solution)/shard_map/ppermute | solution.py:15
  35.4 2.5 %convert_subtract_fusion = f32[128,128]{0,1:T(8,128)S(1)} fusion(f32[1,128,128]{1,2,0:T(8,128)S(1)} %collective-permute-done.4, f32[1,128,128]{1,2,0:T(8,128)S(1)} %collective-permute-done.3, f32[1,128,128]{1,2,0:T(8,128)S(1)} %collective-permute-done.2, bf16[1,128,128]{1,2,0:T(8,128)(2,1)S(1)} %copy.17, f32[]{:T(128)} %bitcast.22, f32[]{:T(128)} %bitcast.20, ...), kind=kLoop, calls=%fused_computation.36 | loop fusion | flops 163840 | bytes 426004 | tf_op jit(solution)/shard_map/sub | solution.py:63
  37.9 5.8 %all-gather = f32[512,128]{0,1:T(8,128)S(1)} all-gather(f32[128,128]{0,1:T(8,128)S(1)} %convert_subtract_fusion), channel_id=2, replica_groups=mesh['tiles'=8,'freq'=4] {'freq'}, dimensions={0}, use_global_device_ids=true | all-gather | bytes 327680 | tf_op jit(solution)/shard_map/all_gather | solution.py:76
  43.7 0.1 reshape.147
  43.8 0.6 fusion.32
  44.3 0.1 copy.22
  44.4 0.3 collective-permute-start.5
  44.7 0.1 copy.18
  44.9 3.6 %collective-permute-done.5 = bf16[128,128]{1,0:T(8,128)(2,1)S(1)} collective-permute-done((bf16[128,128]{1,0:T(8,128)(2,1)S(1)}, bf16[128,128]{1,0:T(8,128)(2,1)S(1)}, u32[]{:S(2)}, u32[]{:S(2)}) %collective-permute-start.5) | collective-permute-done | bytes 32800 | tf_op jit(solution)/shard_map/ppermute | solution.py:26
  48.4 0.2 fusion.14
  48.6 0.1 fusion.1
  48.7 0.1 pad_maximum_fusion
  48.8 0.7 broadcast.86
  49.5 0.6 constant_dynamic-update-slice_fusion
  50.1 3.4 %all-to-all-start.1 = ((bf16[8,64,128]{2,1,0:T(8,128)(2,1)}), bf16[8,64,128]{2,1,0:T(8,128)(2,1)S(1)}, u32[]{:S(2)}, u32[]{:S(2)}) async-start(bf16[8,64,128]{2,1,0:T(8,128)(2,1)} %constant_dynamic-update-slice_fusion), calls=%async_computation.1 | async-start | bytes 262144 | tf_op jit(solution)/shard_map/all_to_all | solution.py:122
  53.5 7.3 %all-to-all-done.1 = bf16[8,64,128]{2,1,0:T(8,128)(2,1)S(1)} async-done(((bf16[8,64,128]{2,1,0:T(8,128)(2,1)}), bf16[8,64,128]{2,1,0:T(8,128)(2,1)S(1)}, u32[]{:S(2)}, u32[]{:S(2)}) %all-to-all-start.1) | async-done | bytes 131104 | tf_op jit(solution)/shard_map/all_to_all | solution.py:122
  60.8 0.6 gather_fusion
  61.3 0.1 broadcast_select_fusion
  61.4 0.1 slice_negate_fusion
  61.5 0.2 copy-done.1
  61.7 0.3 convolution_bitcast_fusion
  61.9 0.3 collective-permute-start.6
  62.2 0.7 %copy.20 = f32[1,128,128]{2,1,0:T(8,128)} copy(f32[1,128,128]{1,2,0:T(8,128)S(1)} %bitcast.90) | data formatting | bytes 131072
  63.0 3.3 %collective-permute-done.6 = f32[128,128]{0,1:T(8,128)S(1)} collective-permute-done((f32[128,128]{0,1:T(8,128)S(1)}, f32[128,128]{0,1:T(8,128)S(1)}, u32[]{:S(2)}, u32[]{:S(2)}) %collective-permute-start.6) | collective-permute-done | bytes 65568 | tf_op jit(solution)/shard_map/ppermute | solution.py:26
  66.3 0.7 %copy.21 = f32[1,128,128]{2,1,0:T(8,128)} copy(f32[1,128,128]{1,2,0:T(8,128)S(1)} %fusion.25) | data formatting | bytes 131072
  (24 shorter events, 0.3 us)
Async XLA Ops:
  0.6 5.4 %collective-permute-start = (bf16[128,128]{1,0:T(8,128)(2,1)}, bf16[128,128]{1,0:T(8,128)(2,1)S(1)}, u32[]{:S(2)}, u32[]{:S(2)}) collective-permute-start(bf16[128,128]{1,0:T(8,128)(2,1)} %bitcast.104), channel_id=1, source_target_pairs={{0,4},{4,0},{8,12},{12,8},{16,20},{20,16},{24,28},{28,24},{1,5},{5... | collective-permute-start | bytes 98312 | tf_op jit(solution)/shard_map/ppermute | solution.py:26
  3.7 0.7 copy-start.4
  4.3 0.7 copy-start.6
  5.1 1.0 %copy-start.5 = (bf16[1,128,128]{2,1,0:T(8,128)(2,1)S(1)}, bf16[1,128,128]{2,1,0:T(8,128)(2,1)}, u32[]{:S(2)}) copy-start(bf16[1,128,128]{2,1,0:T(8,128)(2,1)} %param.7) | copy-start | bytes 98308
  9.0 13.4 %all-to-all-start = ((bf16[8,64,128]{2,1,0:T(8,128)(2,1)}), bf16[8,64,128]{2,1,0:T(8,128)(2,1)S(1)}, u32[]{:S(2)}, u32[]{:S(2)}) async-start(bf16[8,64,128]{2,1,0:T(8,128)(2,1)} %scatter_fusion), calls=%async_computation | async-start | bytes 262144 | tf_op jit(solution)/shard_map/all_to_all | solution.py:103
  22.4 0.9 %copy-start = (bf16[1,1,2,256,128]{4,3,2,1,0:T(8,128)(2,1)S(1)}, bf16[1,1,2,256,128]{4,3,2,1,0:T(8,128)(2,1)}, u32[]{:S(2)}) copy-start(bf16[1,1,2,256,128]{4,3,2,1,0:T(8,128)(2,1)} %param.10) | copy-start | bytes 393220
  23.6 4.3 %collective-permute-start.1 = (f32[128,128]{0,1:T(8,128)S(1)}, f32[128,128]{0,1:T(8,128)S(1)}, u32[]{:S(2)}, u32[]{:S(2)}) collective-permute-start(f32[128,128]{0,1:T(8,128)S(1)} %dynamic-slice_bitcast_fusion.2), channel_id=1, source_target_pairs={{0,4},{4,0},{8,12},{12,8},{16,20},{20,16},{24,28},{28,24},{1,5},{5... | collective-permute-start | bytes 196616 | tf_op jit(solution)/shard_map/ppermute | solution.py:26
  27.9 3.7 %collective-permute-start.3 = (f32[1,128,128]{1,2,0:T(8,128)S(1)}, f32[1,128,128]{1,2,0:T(8,128)S(1)}, u32[]{:S(2)}, u32[]{:S(2)}) collective-permute-start(f32[1,128,128]{1,2,0:T(8,128)S(1)} %fusion.28), channel_id=1, source_target_pairs={{0,1},{1,2},{2,3},{3,0},{4,5},{5,6},{6,7},{7,4},{8,9},{9,10},{10,1... | collective-permute-start | bytes 196616 | tf_op jit(solution)/shard_map/ppermute | solution.py:15
  28.0 5.9 %collective-permute-start.2 = (f32[1,128,128]{1,2,0:T(8,128)S(1)}, f32[1,128,128]{1,2,0:T(8,128)S(1)}, u32[]{:S(2)}, u32[]{:S(2)}) collective-permute-start(f32[1,128,128]{1,2,0:T(8,128)S(1)} %fusion.28), channel_id=1, source_target_pairs={{0,3},{1,0},{2,1},{3,2},{4,7},{5,4},{6,5},{7,6},{8,11},{9,8},{10,9... | collective-permute-start | bytes 196616 | tf_op jit(solution)/shard_map/ppermute | solution.py:17
  31.7 3.7 %collective-permute-start.4 = (f32[1,128,128]{1,2,0:T(8,128)S(1)}, f32[1,128,128]{1,2,0:T(8,128)S(1)}, u32[]{:S(2)}, u32[]{:S(2)}) collective-permute-start(f32[1,128,128]{1,2,0:T(8,128)S(1)} %collective-permute-done.3), channel_id=1, source_target_pairs={{0,1},{1,2},{2,3},{3,0},{4,5},{5,6},{6,7},{7,4},{8,9},{9,10},{10,1... | collective-permute-start | bytes 196616 | tf_op jit(solution)/shard_map/ppermute | solution.py:15
  31.7 0.8 %copy-start.2 = (bf16[1,128,128]{2,1,0:T(8,128)(2,1)S(1)}, bf16[1,128,128]{2,1,0:T(8,128)(2,1)}, u32[]{:S(2)}) copy-start(bf16[1,128,128]{2,1,0:T(8,128)(2,1)} %param.8) | copy-start | bytes 98308
  32.4 0.7 %copy-start.3 = (f32[4,4]{1,0:T(4,128)S(1)}, f32[4,4]{1,0:T(4,128)}, u32[]{:S(2)}) copy-start(f32[4,4]{1,0:T(4,128)} %param.13) | copy-start | bytes 196
  44.4 4.0 %collective-permute-start.5 = (bf16[128,128]{1,0:T(8,128)(2,1)S(1)}, bf16[128,128]{1,0:T(8,128)(2,1)S(1)}, u32[]{:S(2)}, u32[]{:S(2)}) collective-permute-start(bf16[128,128]{1,0:T(8,128)(2,1)S(1)} %bitcast.102), channel_id=1, source_target_pairs={{0,4},{4,0},{8,12},{12,8},{16,20},{20,16},{24,28},{28,24},{1,5},{5... | collective-permute-start | bytes 98312 | tf_op jit(solution)/shard_map/ppermute | solution.py:26
  50.1 10.7 %all-to-all-start.1 = ((bf16[8,64,128]{2,1,0:T(8,128)(2,1)}), bf16[8,64,128]{2,1,0:T(8,128)(2,1)S(1)}, u32[]{:S(2)}, u32[]{:S(2)}) async-start(bf16[8,64,128]{2,1,0:T(8,128)(2,1)} %constant_dynamic-update-slice_fusion), calls=%async_computation.1 | async-start | bytes 262144 | tf_op jit(solution)/shard_map/all_to_all | solution.py:122
  60.8 0.9 %copy-start.1 = (bf16[1,1,2,256,128]{4,3,2,1,0:T(8,128)(2,1)S(1)}, bf16[1,1,2,256,128]{4,3,2,1,0:T(8,128)(2,1)}, u32[]{:S(2)}) copy-start(bf16[1,1,2,256,128]{4,3,2,1,0:T(8,128)(2,1)} %param.9) | copy-start | bytes 393220
  61.9 4.3 %collective-permute-start.6 = (f32[128,128]{0,1:T(8,128)S(1)}, f32[128,128]{0,1:T(8,128)S(1)}, u32[]{:S(2)}, u32[]{:S(2)}) collective-permute-start(f32[128,128]{0,1:T(8,128)S(1)} %dynamic-slice_bitcast_fusion), channel_id=1, source_target_pairs={{0,4},{4,0},{8,12},{12,8},{16,20},{20,16},{24,28},{28,24},{1,5},{5... | collective-permute-start | bytes 196616 | tf_op jit(solution)/shard_map/ppermute | solution.py:26
